TPU v7x, 32 devices: a whole 2x2x4 slice. The times are simulated.
32 devices in a mesh: dp: 8 (over z, x), seq: 4 (over y, core).
Axes of the slice: x: 2, y: 2, z: 4, core: 2. Of those that a mesh axis runs over, the one named last changes fastest.
Arguments:
- captions: bfloat16 [96, 128, 768], P(('dp', 'seq')), may hold values from -6 to 6
- images: bfloat16 [96, 196, 768], P('dp'), may hold values from -6 to 6
- tissue_mask: int32 [96, 196], P('dp'), may hold values from 0 to 1, as said below
- gain_self: bfloat16 [768], P(('dp', 'seq')), may hold values from 0.5 to 1.5
- gain_cross: bfloat16 [768], P(('dp', 'seq')), may hold values from 0.5 to 1.5
- gain_mlp: bfloat16 [768], P(('dp', 'seq')), may hold values from 0.5 to 1.5
- w_qkv: bfloat16 [768, 2304], P(('dp', 'seq')), may hold values from -0.21875 to 0.21875
- w_self_out: bfloat16 [768, 768], P(('dp', 'seq')), may hold values from -0.625 to 0.625
- w_cross_q: bfloat16 [768, 768], P(('dp', 'seq')), may hold values from -0.21875 to 0.21875
- w_cross_kv: bfloat16 [768, 1536], P(('dp', 'seq')), may hold values from -0.21875 to 0.21875
- w_cross_out: bfloat16 [768, 768], P(('dp', 'seq')), may hold values from -0.625 to 0.625
- w_up: bfloat16 [768, 3072], P(('dp', 'seq')), may hold values from -0.21875 to 0.21875
- w_down: bfloat16 [3072, 768], P(('dp', 'seq')), may hold values from -0.109375 to 0.109375
- cotangent: bfloat16 [96, 128, 768], P(('dp', 'seq')), may hold values from -6 to 6
Outputs:
- block_out: bfloat16 [96, 128, 768], P(('dp', 'seq'))
- grad_captions: float32 [96, 128, 768], P(('dp', 'seq'))
- grad_images: float32 [96, 196, 768], P('dp', None, 'seq')
- grad_gain_self: float32 [768], P(('dp', 'seq'))
- grad_gain_cross: float32 [768], P(('dp', 'seq'))
- grad_gain_mlp: float32 [768], P(('dp', 'seq'))
- grad_w_qkv: float32 [768, 2304], P(('dp', 'seq'))
- grad_w_self_out: float32 [768, 768], P(('dp', 'seq'))
- grad_w_cross_q: float32 [768, 768], P(('dp', 'seq'))
- grad_w_cross_kv: float32 [768, 1536], P(('dp', 'seq'))
- grad_w_cross_out: float32 [768, 768], P(('dp', 'seq'))
- grad_w_up: float32 [768, 3072], P(('dp', 'seq'))
- grad_w_down: float32 [3072, 768], P(('dp', 'seq'))
Inputs may be any that keep to these rules, and one draw needn't show every extreme that they name: `tissue_mask`: at least 65 of every image's patches are valid; the valid ones lie anywhere among its 196 slots and their number differs from image to image.
All inputs are finite; a program needn't handle non-finite values.
Results may differ from a plain program's by a relative error of at most 0.019.
Values may be sent and summed in bfloat16 or wider, within the bound.
A program may use at most 192 MiB of HBM per device.

v0:
```python
import jax
import jax.numpy as jnp
from jax import lax
from jax.sharding import PartitionSpec as P

HEADS = 12
HEAD = 64
epsilon = 1e-05


def layer_norm(inputs, gain_vector):
    centered = inputs - jnp.mean(inputs, axis=-1, keepdims=True)
    spread = jnp.mean(centered * centered, axis=-1, keepdims=True)
    return centered * lax.rsqrt(spread + epsilon) * gain_vector


def norm_back(inputs, gain_vector, upstream):
    unused, pullback = jax.vjp(layer_norm, inputs, gain_vector)
    return pullback(upstream)


def exact_gelu(inputs):
    return jax.nn.gelu(inputs, approximate=False)


def linear(inputs, matrix):
    return jnp.einsum("btd,de->bte", inputs, matrix, preferred_element_type=jnp.float32)


def linear_back(upstream, matrix):
    return jnp.einsum("bte,de->btd", upstream, matrix, preferred_element_type=jnp.float32)


def weight_grad(inputs, upstream):
    return jnp.einsum("btd,bte->de", inputs, upstream, preferred_element_type=jnp.float32)


def masked_scores(query_heads, key_heads, allowed, factor):
    raw_scores = (
        jnp.einsum("bqhe,bkhe->bhqk", query_heads, key_heads, preferred_element_type=jnp.float32)
        * factor
    )
    return jnp.where(allowed, raw_scores, -1e30)


def attend_forward(query_heads, key_heads, value_heads, allowed, factor):
    scores = masked_scores(query_heads, key_heads, allowed, factor)
    top_score = jnp.max(scores, axis=-1, keepdims=True)
    exponent = jnp.exp(scores - top_score)
    totals = jnp.sum(exponent, axis=-1, keepdims=True)
    probabilities = (exponent / totals).astype(jnp.bfloat16)
    attended = jnp.einsum(
        "bhqk,bkhe->bqhe", probabilities, value_heads, preferred_element_type=jnp.float32
    )
    return (attended.astype(jnp.bfloat16), top_score + jnp.log(totals))


def attend_back(query_heads, key_heads, value_heads, allowed, factor, log_totals, upstream):
    probabilities = jnp.exp(masked_scores(query_heads, key_heads, allowed, factor) - log_totals)
    grad_probs = jnp.einsum(
        "bqhe,bkhe->bhqk", upstream, value_heads, preferred_element_type=jnp.float32
    )
    centered = grad_probs - jnp.sum(grad_probs * probabilities, axis=-1, keepdims=True)
    grad_scores = (probabilities * centered * factor).astype(jnp.bfloat16)
    grad_queries = jnp.einsum(
        "bhqk,bkhe->bqhe", grad_scores, key_heads, preferred_element_type=jnp.float32
    )
    grad_keys = jnp.einsum(
        "bhqk,bqhe->bkhe", grad_scores, query_heads, preferred_element_type=jnp.float32
    )
    grad_values = jnp.einsum(
        "bhqk,bqhe->bkhe",
        probabilities.astype(jnp.bfloat16),
        upstream,
        preferred_element_type=jnp.float32,
    )
    return (
        grad_queries.astype(jnp.bfloat16),
        grad_keys.astype(jnp.bfloat16),
        grad_values.astype(jnp.bfloat16),
    )


def pair_columns(full_cross_kv, seq_index, head_span, model_width):
    key_cols = lax.dynamic_slice_in_dim(full_cross_kv, seq_index * head_span, head_span, 1)
    value_cols = lax.dynamic_slice_in_dim(
        full_cross_kv, model_width + seq_index * head_span, head_span, 1
    )
    return jnp.concatenate([key_cols, value_cols], axis=1)


def on_device(
    captions,
    images,
    tissue_mask,
    gain_self,
    gain_cross,
    gain_mlp,
    w_qkv,
    w_self_out,
    w_cross_q,
    w_cross_kv,
    w_cross_out,
    w_up,
    w_down,
    cotangent,
):
    groups = lax.axis_size("seq")
    seq_index = lax.axis_index("seq")
    count_local, full_len, model_width = captions.shape
    count_caps = count_local * groups
    patch_count = images.shape[1]
    local_heads = HEADS // groups
    head_span = local_heads * HEAD
    factor = HEAD ** (-0.5)
    gathered = (
        lax.all_gather(gain_self, ("dp", "seq"), axis=0, tiled=True),
        lax.all_gather(gain_cross, ("dp", "seq"), axis=0, tiled=True),
        lax.all_gather(gain_mlp, ("dp", "seq"), axis=0, tiled=True),
        lax.all_gather(w_qkv, ("dp", "seq"), axis=0, tiled=True),
        lax.all_gather(w_self_out, ("dp", "seq"), axis=0, tiled=True),
        lax.all_gather(w_cross_q, ("dp", "seq"), axis=0, tiled=True),
        lax.all_gather(w_cross_kv, ("dp", "seq"), axis=0, tiled=True),
        lax.all_gather(w_cross_out, ("dp", "seq"), axis=0, tiled=True),
        lax.all_gather(w_up, ("dp", "seq"), axis=0, tiled=True),
        lax.all_gather(w_down, ("dp", "seq"), axis=0, tiled=True),
    )
    (
        gain_one,
        gain_two,
        gain_three,
        full_qkv,
        full_self_out,
        full_cross_q,
        full_cross_kv,
        full_cross_out,
        full_up,
        full_down,
    ) = gathered
    position = jnp.arange(full_len)
    causal = (position[:, None] >= position[None, :])[None, None]
    split_shape = (count_local, full_len, groups, head_span)
    head_shape = (count_caps, full_len, local_heads, HEAD)
    back_shape = (count_caps, full_len, 1, head_span)
    token_shape = (count_local, full_len, model_width)
    tokens = captions.astype(jnp.float32)
    normed_one = layer_norm(tokens, gain_one.astype(jnp.float32)).astype(jnp.bfloat16)
    packed = linear(normed_one, full_qkv).astype(jnp.bfloat16)
    query_part = packed[..., :model_width].reshape(split_shape)
    key_part = packed[..., model_width : 2 * model_width].reshape(split_shape)
    value_part = packed[..., 2 * model_width :].reshape(split_shape)
    query_recv, key_recv, value_recv = (
        lax.all_to_all(query_part, "seq", split_axis=2, concat_axis=0, tiled=True),
        lax.all_to_all(key_part, "seq", split_axis=2, concat_axis=0, tiled=True),
        lax.all_to_all(value_part, "seq", split_axis=2, concat_axis=0, tiled=True),
    )
    query_heads = query_recv.reshape(head_shape)
    key_heads = key_recv.reshape(head_shape)
    value_heads = value_recv.reshape(head_shape)
    self_result, self_totals = attend_forward(query_heads, key_heads, value_heads, causal, factor)
    self_back = lax.all_to_all(
        self_result.reshape(back_shape), "seq", split_axis=0, concat_axis=2, tiled=True
    )
    self_tokens = self_back.reshape(token_shape)
    after_self = tokens + linear(self_tokens, full_self_out)
    normed_two = layer_norm(after_self, gain_two.astype(jnp.float32)).astype(jnp.bfloat16)
    cross_full = linear(normed_two, full_cross_q).astype(jnp.bfloat16)
    cross_queries = lax.all_to_all(
        cross_full.reshape(split_shape), "seq", split_axis=2, concat_axis=0, tiled=True
    ).reshape(head_shape)
    image_allowed = (tissue_mask > 0)[:, None, None, :]
    local_pairs = pair_columns(full_cross_kv, seq_index, head_span, model_width)
    image_pairs = linear(images, local_pairs).astype(jnp.bfloat16)
    image_shape = (count_caps, patch_count, local_heads, HEAD)
    cross_keys = image_pairs[..., :head_span].reshape(image_shape)
    cross_values = image_pairs[..., head_span:].reshape(image_shape)
    cross_result, cross_totals = attend_forward(
        cross_queries, cross_keys, cross_values, image_allowed, factor
    )
    cross_back = lax.all_to_all(
        cross_result.reshape(back_shape), "seq", split_axis=0, concat_axis=2, tiled=True
    )
    cross_tokens = cross_back.reshape(token_shape)
    after_cross = after_self + linear(cross_tokens, full_cross_out)
    normed_three = layer_norm(after_cross, gain_three.astype(jnp.float32)).astype(jnp.bfloat16)
    hidden = linear(normed_three, full_up)
    active = exact_gelu(hidden).astype(jnp.bfloat16)
    block_out = (after_cross + linear(active, full_down)).astype(jnp.bfloat16)
    backward_set = (
        lax.all_gather(gain_self, ("dp", "seq"), axis=0, tiled=True),
        lax.all_gather(gain_cross, ("dp", "seq"), axis=0, tiled=True),
        lax.all_gather(gain_mlp, ("dp", "seq"), axis=0, tiled=True),
        lax.all_gather(w_qkv, ("dp", "seq"), axis=0, tiled=True),
        lax.all_gather(w_self_out, ("dp", "seq"), axis=0, tiled=True),
        lax.all_gather(w_cross_q, ("dp", "seq"), axis=0, tiled=True),
        lax.all_gather(w_cross_kv, ("dp", "seq"), axis=0, tiled=True),
        lax.all_gather(w_cross_out, ("dp", "seq"), axis=0, tiled=True),
        lax.all_gather(w_up, ("dp", "seq"), axis=0, tiled=True),
        lax.all_gather(w_down, ("dp", "seq"), axis=0, tiled=True),
    )
    (
        gain_one,
        gain_two,
        gain_three,
        full_qkv,
        full_self_out,
        full_cross_q,
        full_cross_kv,
        full_cross_out,
        full_up,
        full_down,
    ) = backward_set
    grad_down = weight_grad(active, cotangent)
    grad_active = linear_back(cotangent, full_down)
    unused, gelu_pull = jax.vjp(exact_gelu, hidden)
    grad_hidden = gelu_pull(grad_active)[0].astype(jnp.bfloat16)
    grad_up = weight_grad(normed_three, grad_hidden)
    grad_normed_three = linear_back(grad_hidden, full_up)
    norm_grad_three, grad_gain_three = norm_back(
        after_cross, gain_three.astype(jnp.float32), grad_normed_three
    )
    grad_after_cross = cotangent.astype(jnp.float32) + norm_grad_three
    cross_branch = grad_after_cross.astype(jnp.bfloat16)
    grad_cross_out = weight_grad(cross_tokens, cross_branch)
    cross_full_grad = linear_back(cross_branch, full_cross_out).astype(jnp.bfloat16)
    cross_upstream = lax.all_to_all(
        cross_full_grad.reshape(split_shape), "seq", split_axis=2, concat_axis=0, tiled=True
    ).reshape(head_shape)
    grad_cross_queries, grad_cross_keys, grad_cross_values = attend_back(
        cross_queries, cross_keys, cross_values, image_allowed, factor, cross_totals, cross_upstream
    )
    pair_grads = jnp.concatenate(
        [
            grad_cross_keys.reshape(count_caps, patch_count, head_span),
            grad_cross_values.reshape(count_caps, patch_count, head_span),
        ],
        axis=-1,
    )
    local_pairs = pair_columns(full_cross_kv, seq_index, head_span, model_width)
    grad_local_pairs = weight_grad(images, pair_grads)
    image_terms = linear_back(pair_grads, local_pairs)
    grad_images = lax.psum_scatter(
        image_terms.astype(jnp.bfloat16), "seq", scatter_dimension=2, tiled=True
    ).astype(jnp.float32)
    grad_cross_kv = jnp.zeros((model_width, 2 * model_width), jnp.float32)
    grad_cross_kv = lax.dynamic_update_slice_in_dim(
        grad_cross_kv, grad_local_pairs[:, :head_span], seq_index * head_span, 1
    )
    grad_cross_kv = lax.dynamic_update_slice_in_dim(
        grad_cross_kv, grad_local_pairs[:, head_span:], model_width + seq_index * head_span, 1
    )
    query_grad_back = lax.all_to_all(
        grad_cross_queries.reshape(back_shape), "seq", split_axis=0, concat_axis=2, tiled=True
    )
    query_grad_tokens = query_grad_back.reshape(token_shape)
    grad_cross_q = weight_grad(normed_two, query_grad_tokens)
    grad_normed_two = linear_back(query_grad_tokens, full_cross_q)
    norm_grad_two, grad_gain_two = norm_back(
        after_self, gain_two.astype(jnp.float32), grad_normed_two
    )
    grad_after_self = grad_after_cross + norm_grad_two
    self_branch = grad_after_self.astype(jnp.bfloat16)
    grad_self_out = weight_grad(self_tokens, self_branch)
    self_full_grad = linear_back(self_branch, full_self_out).astype(jnp.bfloat16)
    self_upstream = lax.all_to_all(
        self_full_grad.reshape(split_shape), "seq", split_axis=2, concat_axis=0, tiled=True
    ).reshape(head_shape)
    grad_queries, grad_keys, grad_values = attend_back(
        query_heads, key_heads, value_heads, causal, factor, self_totals, self_upstream
    )
    query_back, key_back, value_back = (
        lax.all_to_all(
            grad_queries.reshape(back_shape), "seq", split_axis=0, concat_axis=2, tiled=True
        ),
        lax.all_to_all(
            grad_keys.reshape(back_shape), "seq", split_axis=0, concat_axis=2, tiled=True
        ),
        lax.all_to_all(
            grad_values.reshape(back_shape), "seq", split_axis=0, concat_axis=2, tiled=True
        ),
    )
    packed_grad = jnp.concatenate(
        [
            query_back.reshape(token_shape),
            key_back.reshape(token_shape),
            value_back.reshape(token_shape),
        ],
        axis=-1,
    )
    grad_qkv = weight_grad(normed_one, packed_grad)
    grad_normed_one = linear_back(packed_grad, full_qkv)
    norm_grad_one, grad_gain_one = norm_back(tokens, gain_one.astype(jnp.float32), grad_normed_one)
    grad_captions = grad_after_self + norm_grad_one
    shards = (
        lax.psum_scatter(grad_gain_one, ("dp", "seq"), scatter_dimension=0, tiled=True),
        lax.psum_scatter(grad_gain_two, ("dp", "seq"), scatter_dimension=0, tiled=True),
        lax.psum_scatter(grad_gain_three, ("dp", "seq"), scatter_dimension=0, tiled=True),
        lax.psum_scatter(grad_qkv, ("dp", "seq"), scatter_dimension=0, tiled=True),
        lax.psum_scatter(grad_self_out, ("dp", "seq"), scatter_dimension=0, tiled=True),
        lax.psum_scatter(grad_cross_q, ("dp", "seq"), scatter_dimension=0, tiled=True),
        lax.psum_scatter(grad_cross_kv, ("dp", "seq"), scatter_dimension=0, tiled=True),
        lax.psum_scatter(grad_cross_out, ("dp", "seq"), scatter_dimension=0, tiled=True),
        lax.psum_scatter(grad_up, ("dp", "seq"), scatter_dimension=0, tiled=True),
        lax.psum_scatter(grad_down, ("dp", "seq"), scatter_dimension=0, tiled=True),
    )
    return (
        block_out,
        grad_captions,
        grad_images,
        shards[0],
        shards[1],
        shards[2],
        shards[3],
        shards[4],
        shards[5],
        shards[6],
        shards[7],
        shards[8],
        shards[9],
    )


def solution(mesh):
    return jax.shard_map(
        on_device,
        mesh=mesh,
        in_specs=(
            P(("dp", "seq"), None, None),
            P("dp", None, None),
            P("dp", None),
            P(("dp", "seq")),
            P(("dp", "seq")),
            P(("dp", "seq")),
            P(("dp", "seq"), None),
            P(("dp", "seq"), None),
            P(("dp", "seq"), None),
            P(("dp", "seq"), None),
            P(("dp", "seq"), None),
            P(("dp", "seq"), None),
            P(("dp", "seq"), None),
            P(("dp", "seq"), None, None),
        ),
        out_specs=(
            P(("dp", "seq"), None, None),
            P(("dp", "seq"), None, None),
            P("dp", None, "seq"),
            P(("dp", "seq")),
            P(("dp", "seq")),
            P(("dp", "seq")),
            P(("dp", "seq"), None),
            P(("dp", "seq"), None),
            P(("dp", "seq"), None),
            P(("dp", "seq"), None),
            P(("dp", "seq"), None),
            P(("dp", "seq"), None),
            P(("dp", "seq"), None),
        ),
        check_vma=False,
    )
```

profile of v0, /device:TPU:0, one launch (start us, length us, event | category | flops | bytes accessed | tf_op | source)
XLA Modules:
  0.0 1383.9 jit_solution(16979897317913632275)
XLA Ops:
  13.7 42.1 %all-reduce.7 = (bf16[768]{0:T(1024)(128)(2,1)S(1)}, bf16[768]{0:T(1024)(128)(2,1)}, bf16[768]{0:T(1024)(128)(2,1)}) all-reduce(bf16[768]{0:T(1024)(128)(2,1)S(1)} %dynamic-update-slice, bf16[768]{0:T(1024)(128)(2,1)S(1)} %dynamic-update-slice.1, bf16[768]{0:T(1024)(128)(2,1)S(1)} %dynamic-update-slice.2), channel_id=1, replica_groups=mesh['dp'=8,'seq'=4] {'dp','seq'}, use_global_device_ids=true, to_apply=%add | all-reduce | flops 2304 | bytes 9216
  58.6 15.4 %all-gather.8.cloned.1.call-done = bf16[768,2304]{1,0:T(8,128)(2,1)} async-done(((bf16[24,2304]{1,0:T(8,128)(2,1)}), bf16[768,2304]{1,0:T(8,128)(2,1)}) %all-gather.8.cloned.1.call-update) | async-done | bytes 3538960 | tf_op jit(solution)/shard_map/all_gather | solution.py:120
  74.0 3.8 convolution_convert_fusion
  79.2 3.5 all-to-all-start.2
  83.8 8.9 all-to-all-done.2
  92.7 3.5 all-to-all-start.1
  98.7 8.0 all-to-all-done.1
  106.8 4.1 all-to-all-start
  113.3 8.1 all-to-all-done
  121.4 2.4 convolution_convert_fusion.6
  123.9 3.6 all-to-all-start.3
  127.5 5.8 all-gather.12.cloned.1.call-done
  137.1 52.2 %all-gather.10.cloned.1.call-done = bf16[768,768]{1,0:T(8,128)(2,1)} async-done(((bf16[24,768]{1,0:T(8,128)(2,1)}), bf16[768,768]{1,0:T(8,128)(2,1)}) %all-gather.10.cloned.1.call-update) | async-done | bytes 1179664 | tf_op jit(solution)/shard_map/all_gather | solution.py:121
  191.6 53.5 %all-gather.14.cloned.1.call-done = bf16[768,768]{1,0:T(8,128)(2,1)} async-done(((bf16[24,768]{1,0:T(8,128)(2,1)}), bf16[768,768]{1,0:T(8,128)(2,1)}) %all-gather.14.cloned.1.call-update) | async-done | bytes 1179664 | tf_op jit(solution)/shard_map/all_gather | solution.py:122
  248.2 4.4 all-to-all-start.4
  252.6 4.2 convert_bitcast_fusion
  258.3 2.5 copy.148
  262.4 2.8 fusion.132
  269.2 3.9 all-to-all-start.5
  273.1 9.5 all-to-all-done.5
  282.6 18.4 %all-gather.16.cloned.1.call-done = bf16[768,768]{1,0:T(8,128)(2,1)} async-done(((bf16[24,768]{1,0:T(8,128)(2,1)}), bf16[768,768]{1,0:T(8,128)(2,1)}) %all-gather.16.cloned.1.call-update) | async-done | bytes 1179664 | tf_op jit(solution)/shard_map/all_gather | solution.py:124
  305.0 61.3 %all-gather.18.cloned.1.call-done = bf16[768,3072]{1,0:T(8,128)(2,1)} async-done(((bf16[24,3072]{1,0:T(8,128)(2,1)}), bf16[768,3072]{1,0:T(8,128)(2,1)}) %all-gather.18.cloned.1.call-update) | async-done | bytes 4718608 | tf_op jit(solution)/shard_map/all_gather | solution.py:125
  366.3 5.7 fusion.101
  374.2 11.6 multiply_convert_fusion
  385.8 45.8 %all-gather.20.cloned.1.call-done = bf16[3072,768]{1,0:T(8,128)(2,1)} async-done(((bf16[96,768]{1,0:T(8,128)(2,1)}), bf16[3072,768]{1,0:T(8,128)(2,1)}) %all-gather.20.cloned.1.call-update) | async-done | bytes 4718608 | tf_op jit(solution)/shard_map/all_gather | solution.py:126
  431.6 8.2 add_convert_fusion
  439.8 6.0 multiply_reduce_fusion.2
  451.3 3.5 all-to-all-start.6
  455.8 8.5 all-to-all-done.6
  464.3 4.4 fusion.134
  471.0 8.2 fusion.57
  479.3 2.6 copy.171
  483.4 6.7 convolution_convert_fusion.1
  490.2 3.3 convolution_bitcast_fusion.3
  493.6 9.2 fusion.69
  502.8 17.0 %all_to_all.180 = bf16[12,128,1,192]{1,3,2,0:T(8,128)(2,1)S(1)} all-to-all(bf16[12,128,1,192]{1,3,2,0:T(8,128)(2,1)S(1)} %bitcast.236), channel_id=1, replica_groups=mesh['dp'=8,'seq'=4] {'seq'}, dimensions={0} | all-to-all | bytes 1179648 | tf_op jit(solution)/shard_map/all_to_all | solution.py:252
  529.4 4.7 convolution_bitcast_fusion.6
  535.6 2.8 broadcast_in_dim.91
  538.3 4.9 dynamic_update_slice.6
  543.3 4.8 dynamic_update_slice.7
  551.2 3.6 all-to-all-start.8
  556.2 8.1 all-to-all-done.8
  564.3 3.0 fusion.135
  567.3 4.6 fusion.75
  571.9 4.2 all-to-all-start.9
  576.1 4.5 fusion.78
  580.6 5.1 all-to-all-done.9
  585.7 4.1 all-to-all-start.10
  589.9 2.5 convolution_convert_fusion.2
  592.3 9.7 all-to-all-done.10
  602.0 3.5 all-to-all-start.11
  608.6 6.5 all-to-all-done.11
  615.3 5.1 convolution_bitcast_fusion
  621.7 6.9 convolution_bitcast_fusion.2
  629.7 8.0 convolution_bitcast_fusion.1
  637.8 6.0 fusion.72
  646.1 41.3 %all-reduce.6 = (f32[768]{0:T(1024)S(1)}, f32[768]{0:T(1024)S(1)}, f32[768]{0:T(1024)S(1)}) all-reduce(f32[768]{0:T(1024)S(1)} %get-tuple-element.19, f32[768]{0:T(1024)} %get-tuple-element.15, f32[768]{0:T(1024)} %get-tuple-element.17), channel_id=3, replica_groups=mesh['dp'=8,'seq'=4] {'dp','seq'}, use_global_device_ids=true, to_apply=%region_20.21.clone | all-reduce | flops 2304 | bytes 18432
  690.7 2.9 convert_element_type.174
  693.6 58.0 %reduce-scatter.15.cloned.1.call-done = f32[24,768]{1,0:T(8,128)} async-done(((f32[768,768]{1,0:T(8,128)}), f32[24,768]{1,0:T(8,128)}) %reduce-scatter.15.cloned.1.call-update) | async-done | bytes 73744 | tf_op jit(solution)/shard_map/reduce_scatter | solution.py:300
  751.6 104.8 %reduce-scatter.13.cloned.1.call-done = f32[24,768]{1,0:T(8,128)} async-done(((f32[768,768]{1,0:T(8,128)}), f32[24,768]{1,0:T(8,128)}) %reduce-scatter.13.cloned.1.call-update) | async-done | bytes 73744 | tf_op jit(solution)/shard_map/reduce_scatter | solution.py:299
  856.4 111.9 %reduce-scatter.17.cloned.1.call-done = f32[24,1536]{1,0:T(8,128)} async-done(((f32[768,1536]{1,0:T(8,128)}), f32[24,1536]{1,0:T(8,128)}) %reduce-scatter.17.cloned.1.call-update) | async-done | bytes 147472 | tf_op jit(solution)/shard_map/reduce_scatter | solution.py:301
  968.3 125.6 %reduce-scatter.11.cloned.1.call-done = f32[24,2304]{1,0:T(8,128)} async-done(((f32[768,2304]{1,0:T(8,128)}), f32[24,2304]{1,0:T(8,128)}) %reduce-scatter.11.cloned.1.call-update) | async-done | bytes 221200 | tf_op jit(solution)/shard_map/reduce_scatter | solution.py:298
  1093.9 141.2 %reduce-scatter.21.cloned.1.call-done = f32[24,3072]{1,0:T(8,128)} async-done(((f32[768,3072]{1,0:T(8,128)}), f32[24,3072]{1,0:T(8,128)}) %reduce-scatter.21.cloned.1.call-update) | async-done | bytes 294928 | tf_op jit(solution)/shard_map/reduce_scatter | solution.py:303
  1235.1 141.9 %reduce-scatter.23.cloned.1.call-done = f32[96,768]{1,0:T(8,128)} async-done(((f32[3072,768]{1,0:T(8,128)}), f32[96,768]{1,0:T(8,128)}) %reduce-scatter.23.cloned.1.call-update) | async-done | bytes 294928 | tf_op jit(solution)/shard_map/reduce_scatter | solution.py:304
  (241 shorter events, 76.0 us)
Async XLA Ops:
  7.2 66.8 %all-gather.8.cloned.1.call-start = ((), (), s32[]{:S(2)}) async-start(), calls=%async_computation.20 | async-start | bytes 3649536 | tf_op jit(solution)/shard_map/all_gather | solution.py:120
  7.9 125.4 %all-gather.12.cloned.1.call-start = ((), (), s32[]{:S(2)}) async-start(), calls=%async_computation.22 | async-start | bytes 2433024 | tf_op jit(solution)/shard_map/all_gather | solution.py:123
  8.7 180.6 %all-gather.10.cloned.1.call-start = ((), (), s32[]{:S(2)}) async-start(), calls=%async_computation.21 | async-start | bytes 1216512 | tf_op jit(solution)/shard_map/all_gather | solution.py:121
  9.4 235.7 %all-gather.14.cloned.1.call-start = ((), (), s32[]{:S(2)}) async-start(), calls=%async_computation.23 | async-start | bytes 1216512 | tf_op jit(solution)/shard_map/all_gather | solution.py:122
  10.0 291.0 %all-gather.16.cloned.1.call-start = ((), (), s32[]{:S(2)}) async-start(), calls=%async_computation.24 | async-start | bytes 1216512 | tf_op jit(solution)/shard_map/all_gather | solution.py:124
  10.6 355.7 %all-gather.18.cloned.1.call-start = ((), (), s32[]{:S(2)}) async-start(), calls=%async_computation.25 | async-start | bytes 4866048 | tf_op jit(solution)/shard_map/all_gather | solution.py:125
  58.6 19.3 %copy-start.51 = (f32[3,128]{1,0:T(4,128)}, f32[3,128]{1,0:T(4,128)S(1)}, u32[]{:S(2)}) copy-start(f32[3,128]{1,0:T(4,128)S(1)} %fusion.83) | copy-start | bytes 4612
  79.2 13.5 all-to-all-start.2
  92.7 18.2 %copy-start.25 = (bf16[3,128,4,192]{1,3,0,2:T(8,128)(2,1)}, bf16[3,128,4,192]{1,3,0,2:T(8,128)(2,1)S(1)}, u32[]{:S(2)}) copy-start(bf16[3,128,4,192]{1,3,0,2:T(8,128)(2,1)S(1)} %all-to-all-done.2) | copy-start | bytes 1769476
  92.7 14.1 %all-to-all-start.1 = ((bf16[3,128,4,192]{1,3,0,2:T(8,128)(2,1)}), bf16[3,128,4,192]{1,3,0,2:T(8,128)(2,1)S(1)}, u32[]{:S(2)}, u32[]{:S(2)}) async-start(bf16[3,128,4,192]{1,3,0,2:T(8,128)(2,1)} %copy.138), calls=%async_computation.1 | async-start | bytes 1179648 | tf_op jit(solution)/shard_map/all_to_all | solution.py:153
  96.2 335.4 %all-gather.20.cloned.1.call-start = ((), (), s32[]{:S(2)}) async-start(), calls=%async_computation.26 | async-start | bytes 4866048 | tf_op jit(solution)/shard_map/all_gather | solution.py:126
  106.8 5.5 copy-start.26
  106.8 14.7 %all-to-all-start = ((bf16[3,128,4,192]{1,3,0,2:T(8,128)(2,1)}), bf16[3,128,4,192]{1,3,0,2:T(8,128)(2,1)}, u32[]{:S(2)}, u32[]{:S(2)}) async-start(bf16[3,128,4,192]{1,3,0,2:T(8,128)(2,1)} %copy.136), calls=%async_computation | async-start | bytes 1179648 | tf_op jit(solution)/shard_map/all_to_all | solution.py:155
  112.3 11.6 copy-start.3
  113.3 8.1 copy-start.37
  121.4 6.1 copy-start.61
  121.4 6.1 copy-start.59
  123.9 65.4 %copy-start.2 = (bf16[3,128,768]{2,1,0:T(8,128)(2,1)S(1)}, bf16[3,128,768]{2,1,0:T(8,128)(2,1)}, u32[]{:S(2)}) copy-start(bf16[3,128,768]{2,1,0:T(8,128)(2,1)} %param.14) | copy-start | bytes 1769476
  123.9 13.1 all-to-all-start.3
  127.5 117.6 %copy-start.34 = (f32[768]{0:T(1024)}, f32[768]{0:T(1024)S(1)}, u32[]{:S(2)}) copy-start(f32[768]{0:T(1024)S(1)} %convert_element_type.141) | copy-start | bytes 9220
  135.7 116.9 %copy-start.30 = (bf16[768,192]{1,0:T(8,128)(2,1)}, bf16[768,192]{1,0:T(8,128)(2,1)S(1)}, u32[]{:S(2)}) copy-start(bf16[768,192]{1,0:T(8,128)(2,1)S(1)} %get-tuple-element.31) | copy-start | bytes 884740
  137.0 54.5 %copy-start.14 = (bf16[3,128,4,1,192]{1,4,2,0,3:T(8,128)(2,1)}, bf16[3,128,4,1,192]{1,4,2,0,3:T(8,128)(2,1)S(1)}, u32[]{:S(2)}) copy-start(bf16[3,128,4,1,192]{1,4,2,0,3:T(8,128)(2,1)S(1)} %copy.143) | copy-start | bytes 1769476
  191.3 56.1 %copy-start.43 = (f32[3,128]{1,0:T(4,128)}, f32[3,128]{1,0:T(4,128)S(1)}, u32[]{:S(2)}) copy-start(f32[3,128]{1,0:T(4,128)S(1)} %broadcast_multiply_fusion.1) | copy-start | bytes 4612
  191.5 56.7 %copy-start.53 = (f32[3,128]{1,0:T(4,128)}, f32[3,128]{1,0:T(4,128)S(1)}, u32[]{:S(2)}) copy-start(f32[3,128]{1,0:T(4,128)S(1)} %multiply_reduce_fusion.7) | copy-start | bytes 4612
  191.6 56.6 %copy-start.48 = (f32[3,128]{1,0:T(4,128)}, f32[3,128]{1,0:T(4,128)S(1)}, u32[]{:S(2)}) copy-start(f32[3,128]{1,0:T(4,128)S(1)} %fusion.110) | copy-start | bytes 4612
  247.3 5.3 copy-start.31
  248.2 14.2 %all-to-all-start.4 = ((bf16[3,128,4,192]{1,3,0,2:T(8,128)(2,1)}), bf16[3,128,4,192]{1,3,0,2:T(8,128)(2,1)}, u32[]{:S(2)}, u32[]{:S(2)}) async-start(bf16[3,128,4,192]{1,3,0,2:T(8,128)(2,1)} %copy.147), calls=%async_computation.4 | async-start | bytes 1179648 | tf_op jit(solution)/shard_map/all_to_all | solution.py:168
  265.2 4.0 copy-start
  265.2 4.0 copy-start.33
  267.4 5.7 copy-start.60
  269.2 13.4 all-to-all-start.5
  303.0 142.8 %copy-start.5 = (f32[3,128,768]{2,1,0:T(8,128)}, f32[3,128,768]{2,1,0:T(8,128)S(1)}, u32[]{:S(2)}) copy-start(f32[3,128,768]{2,1,0:T(8,128)S(1)} %get-tuple-element.47) | copy-start | bytes 3538948
  431.6 8.2 copy-start.41
  431.6 8.2 copy-start.46
  439.8 6.0 copy-start.28
  439.8 6.0 copy-start.56
  447.5 3.7 copy-start.27
  451.3 13.0 all-to-all-start.6
  454.7 235.9 %reduce-scatter.9.cloned.1.call-start = ((), (), s32[]{:S(2)}) async-start(), calls=%async_computation.27 | async-start | bytes 5898240 | tf_op jit(solution)/shard_map/reduce_scatter | solution.py:242
  455.7 15.3 %copy-start.39 = (f32[12,3,128]{2,1,0:T(4,128)}, f32[12,3,128]{2,1,0:T(4,128)S(1)}, u32[]{:S(2)}) copy-start(f32[12,3,128]{2,1,0:T(4,128)S(1)} %log_add_fusion.1) | copy-start | bytes 55300
  464.3 4.4 copy-start.1
  490.1 203.5 %reduce-scatter.19.cloned.1.call-start = ((), (), s32[]{:S(2)}) async-start(), calls=%async_computation.32 | async-start | bytes 2433024 | tf_op jit(solution)/shard_map/reduce_scatter | solution.py:302
  493.5 258.1 %reduce-scatter.15.cloned.1.call-start = ((), (), s32[]{:S(2)}) async-start(), calls=%async_computation.30 | async-start | bytes 2433024 | tf_op jit(solution)/shard_map/reduce_scatter | solution.py:300
  502.8 17.1 %copy-start.35 = (f32[768]{0:T(1024)S(1)}, f32[768]{0:T(1024)}, u32[]{:S(2)}) copy-start(f32[768]{0:T(1024)} %copy-done.34) | copy-start | bytes 9220
  502.8 17.1 %copy-start.44 = (f32[3,128]{1,0:T(4,128)S(1)}, f32[3,128]{1,0:T(4,128)}, u32[]{:S(2)}) copy-start(f32[3,128]{1,0:T(4,128)} %copy-done.43) | copy-start | bytes 4612
  502.8 17.1 %copy-start.49 = (f32[3,128]{1,0:T(4,128)S(1)}, f32[3,128]{1,0:T(4,128)}, u32[]{:S(2)}) copy-start(f32[3,128]{1,0:T(4,128)} %copy-done.48) | copy-start | bytes 4612
  522.3 3.7 copy-start.12
  522.3 334.1 %reduce-scatter.13.cloned.1.call-start = ((), (), s32[]{:S(2)}) async-start(), calls=%async_computation.29 | async-start | bytes 2433024 | tf_op jit(solution)/shard_map/reduce_scatter | solution.py:299
  527.1 21.0 %copy-start.7 = (f32[3,128,768]{2,1,0:T(8,128)}, f32[3,128,768]{2,1,0:T(8,128)S(1)}, u32[]{:S(2)}) copy-start(f32[3,128,768]{2,1,0:T(8,128)S(1)} %add_add_fusion.4) | copy-start | bytes 3538948
  529.3 439.0 %reduce-scatter.17.cloned.1.call-start = ((), (), s32[]{:S(2)}) async-start(), calls=%async_computation.31 | async-start | bytes 4866048 | tf_op jit(solution)/shard_map/reduce_scatter | solution.py:301
  551.1 16.2 %copy-start.4 = (f32[12,3,128,128]{2,3,1,0:T(8,128)S(1)}, f32[12,3,128,128]{2,3,1,0:T(8,128)}, u32[]{:S(2)}) copy-start(f32[12,3,128,128]{2,3,1,0:T(8,128)} %copy-done.3) | copy-start | bytes 7077892
  551.2 13.1 all-to-all-start.8
  571.9 13.8 all-to-all-start.9
  585.7 16.3 %all-to-all-start.10 = ((bf16[12,128,1,192]{1,3,2,0:T(8,128)(2,1)}), bf16[12,128,1,192]{1,3,2,0:T(8,128)(2,1)}, u32[]{:S(2)}, u32[]{:S(2)}) async-start(bf16[12,128,1,192]{1,3,2,0:T(8,128)(2,1)} %bitcast.234), calls=%async_computation.10 | async-start | bytes 1179648 | tf_op jit(solution)/shard_map/all_to_all | solution.py:275
  602.0 13.0 all-to-all-start.11
  605.5 488.3 %reduce-scatter.11.cloned.1.call-start = ((), (), s32[]{:S(2)}) async-start(), calls=%async_computation.28 | async-start | bytes 7299072 | tf_op jit(solution)/shard_map/reduce_scatter | solution.py:298
  608.5 11.9 copy-start.21
  615.3 5.2 copy-start.23
  620.5 614.6 %reduce-scatter.21.cloned.1.call-start = ((), (), s32[]{:S(2)}) async-start(), calls=%async_computation.33 | async-start | bytes 9732096 | tf_op jit(solution)/shard_map/reduce_scatter | solution.py:303
  628.7 748.3 %reduce-scatter.23.cloned.1.call-start = ((), (), s32[]{:S(2)}) async-start(), calls=%async_computation.34 | async-start | bytes 9732096 | tf_op jit(solution)/shard_map/reduce_scatter | solution.py:304
  637.7 6.1 copy-start.22
  637.7 6.0 copy-start.24
  637.8 6.0 copy-start.62
  645.5 43.7 %copy-start.8 = (f32[3,128,768]{2,1,0:T(8,128)S(1)}, f32[3,128,768]{2,1,0:T(8,128)}, u32[]{:S(2)}) copy-start(f32[3,128,768]{2,1,0:T(8,128)} %copy-done.7) | copy-start | bytes 3538948
  (25 other events, 49.6 us)
Sparse Core Ops, SparseCore 0:
  10.9 63.0 all-gather.7
  76.9 56.3 all-gather.11
  136.2 52.9 all-gather.9
  192.0 53.0 all-gather.13
  247.8 53.0 all-gather.15
  303.7 62.5 all-gather.17
  369.2 62.3 all-gather.19
  490.2 51.1 reduce-scatter.8
  548.2 99.5 reduce-scatter.18
  653.5 98.0 reduce-scatter.14
  758.3 98.0 reduce-scatter.12
  862.3 105.9 reduce-scatter.16
  975.5 118.3 reduce-scatter.10
  1100.2 134.8 reduce-scatter.20
  1242.4 134.4 reduce-scatter.22
where the time goes:
time: 1390 us; the launch traced here: 1380 us
  waiting for transfers between devices  1010 us (73%)
  matrix products  132 us (9%)
  blocking collectives  100 us (7%)
  local copies, waits for them, and re-layouts  52.1 us (4%)
  starting transfers between devices  43.1 us (3%)
  other arithmetic  26.8 us (2%)
  between operations  15.3 us (1%)
    reduce_scatter x1, waiting for transfers between devices, on_device(): lax.psum_scatter(grad_down, ('dp', 'seq'), scatter_dimension=0, tiled=True)  142 us
    reduce_scatter x1, waiting for transfers between devices, on_device(): lax.psum_scatter(grad_up, ('dp', 'seq'), scatter_dimension=0, tiled=True)  141 us
    reduce_scatter x1, waiting for transfers between devices, on_device(): lax.psum_scatter(grad_qkv, ('dp', 'seq'), scatter_dimension=0, tiled=True)  126 us
    reduce_scatter x1, waiting for transfers between devices, on_device(): lax.psum_scatter(grad_cross_kv, ('dp', 'seq'), scatter_dimension=0, tiled...  112 us
    reduce_scatter x1, waiting for transfers between devices, on_device(): lax.psum_scatter(grad_self_out, ('dp', 'seq'), scatter_dimension=0, tiled...  105 us
    unnamed x2, blocking collectives  83.5 us
    all_gather x1, waiting for transfers between devices, on_device(): lax.all_gather(w_up, ('dp', 'seq'), axis=0, tiled=True)  61.3 us
    reduce_scatter x1, waiting for transfers between devices, on_device(): lax.psum_scatter(grad_cross_q, ('dp', 'seq'), scatter_dimension=0, tiled=...  58 us
  transfers between devices with their start and end apart: 26, of which 24 were waited for; matrix products, arithmetic and copies ran while one was open for 11% of the time, Pallas kernels for 0%

commit v1 on v0

--- a/solution.py
+++ b/solution.py
@@ -6,6 +6,22 @@
 HEADS = 12
 HEAD = 64
 epsilon = 1e-05
+
+
+def figure_perform(panel, k_dim):
+    which_axis = ("dp", "seq")
+    big = lax.axis_size(which_axis)
+    mat_out, g_now = (big, lax.axis_index(which_axis))
+    f_next, ready = (panel, 1)
+    while ready < mat_out:
+        wide_out = lax.ppermute(
+            f_next, axis_name=which_axis, perm=[(t, t ^ ready) for t in range(mat_out)]
+        )
+        local_out = jnp.concatenate([f_next, wide_out], axis=k_dim)
+        local_next = jnp.concatenate([wide_out, f_next], axis=k_dim)
+        f_next = jnp.where(g_now & ready == 0, local_out, local_next)
+        ready = 2 * ready
+    return f_next
 
 
 def layer_norm(inputs, gain_vector):
@@ -119,7 +135,7 @@
         lax.all_gather(gain_mlp, ("dp", "seq"), axis=0, tiled=True),
         lax.all_gather(w_qkv, ("dp", "seq"), axis=0, tiled=True),
         lax.all_gather(w_self_out, ("dp", "seq"), axis=0, tiled=True),
-        lax.all_gather(w_cross_q, ("dp", "seq"), axis=0, tiled=True),
+        figure_perform(w_cross_q, k_dim=0),
         lax.all_gather(w_cross_kv, ("dp", "seq"), axis=0, tiled=True),
         lax.all_gather(w_cross_out, ("dp", "seq"), axis=0, tiled=True),
         lax.all_gather(w_up, ("dp", "seq"), axis=0, tiled=True),

time: 1390 us -> 1340 us (0.964)
  waiting for transfers between devices: 1010 us -> 953 us
    all_gather x1, waiting for transfers between devices: 53.5 us -> 0.02 us  [on_device(): lax.all_gather(w_cross_q, ('dp', 'seq'), axis=0, tiled=True)]
  transfers between devices with their start and end apart: 26 -> 31, of which waited for: 24 -> 24; matrix products, arithmetic and copies ran while one was open for 11% -> 16% of each run, Pallas kernels for 0% -> 0%
where the time goes in v1:
time: 1340 us; the launch traced here: 1330 us
  waiting for transfers between devices  953 us (71%)
  matrix products  134 us (10%)
  blocking collectives  101 us (8%)
  local copies, waits for them, and re-layouts  53.7 us (4%)
  starting transfers between devices  47.4 us (4%)
  other arithmetic  30.9 us (2%)
  between operations  15.3 us (1%)
    reduce_scatter x1, waiting for transfers between devices, on_device(): lax.psum_scatter(grad_down, ('dp', 'seq'), scatter_dimension=0, tiled=True)  142 us
    reduce_scatter x1, waiting for transfers between devices, on_device(): lax.psum_scatter(grad_up, ('dp', 'seq'), scatter_dimension=0, tiled=True)  141 us
    reduce_scatter x1, waiting for transfers between devices, on_device(): lax.psum_scatter(grad_qkv, ('dp', 'seq'), scatter_dimension=0, tiled=True)  126 us
    reduce_scatter x1, waiting for transfers between devices, on_device(): lax.psum_scatter(grad_cross_kv, ('dp', 'seq'), scatter_dimension=0, tiled...  112 us
    reduce_scatter x1, waiting for transfers between devices, on_device(): lax.psum_scatter(grad_self_out, ('dp', 'seq'), scatter_dimension=0, tiled...  105 us
    unnamed x2, blocking collectives  83.5 us
    all_gather x1, waiting for transfers between devices, on_device(): lax.all_gather(w_up, ('dp', 'seq'), axis=0, tiled=True)  61.3 us
    reduce_scatter x1, waiting for transfers between devices, on_device(): lax.psum_scatter(grad_cross_q, ('dp', 'seq'), scatter_dimension=0, tiled=...  57 us
  transfers between devices with their start and end apart: 31, of which 24 were waited for; matrix products, arithmetic and copies ran while one was open for 16% of the time, Pallas kernels for 0%

profile of v1, /device:TPU:0, one launch (start us, length us, event | category | flops | bytes accessed | tf_op | source)
XLA Modules:
  0.0 1334.7 jit_solution(1087082328544958652)
XLA Ops:
  13.7 42.1 %all-reduce.7 = (bf16[768]{0:T(1024)(128)(2,1)S(1)}, bf16[768]{0:T(1024)(128)(2,1)S(1)}, bf16[768]{0:T(1024)(128)(2,1)}) all-reduce(bf16[768]{0:T(1024)(128)(2,1)S(1)} %dynamic-update-slice, bf16[768]{0:T(1024)(128)(2,1)S(1)} %dynamic-update-slice.1, bf16[768]{0:T(1024)(128)(2,1)S(1)} %dynamic-update-slice.2), channel_id=1, replica_groups=mesh['dp'=8,'seq'=4] {'dp','seq'}, use_global_device_ids=true, to_apply=%add | all-reduce | flops 2304 | bytes 9216
  58.6 15.4 %all-gather.8.cloned.1.call-done = bf16[768,2304]{1,0:T(8,128)(2,1)} async-done(((bf16[24,2304]{1,0:T(8,128)(2,1)}), bf16[768,2304]{1,0:T(8,128)(2,1)}) %all-gather.8.cloned.1.call-update) | async-done | bytes 3538960 | tf_op jit(solution)/shard_map/all_gather | solution.py:136
  74.0 3.8 convolution_convert_fusion
  79.2 3.5 all-to-all-start.2
  87.1 6.1 all-to-all-done.2
  93.2 3.5 all-to-all-start.1
  98.8 4.7 collective-permute-done.2
  107.2 4.2 all-to-all-start
  113.8 8.3 all-to-all-done
  124.5 3.6 all-to-all-start.3
  130.3 3.3 all-gather.12.cloned.1.call-done
  133.6 2.5 constant_dynamic-slice_fusion.1
  137.7 54.6 %all-gather.10.cloned.1.call-done = bf16[768,768]{1,0:T(8,128)(2,1)} async-done(((bf16[24,768]{1,0:T(8,128)(2,1)}), bf16[768,768]{1,0:T(8,128)(2,1)}) %all-gather.10.cloned.1.call-update) | async-done | bytes 1179664 | tf_op jit(solution)/shard_map/all_gather | solution.py:137
  199.0 4.4 all-to-all-start.4
  203.4 4.2 convert_bitcast_fusion
  213.1 2.8 fusion.140
  219.8 3.5 all-to-all-start.5
  224.1 8.7 all-to-all-done.5
  232.9 15.3 %all-gather.14.cloned.1.call-done = bf16[768,768]{1,0:T(8,128)(2,1)} async-done(((bf16[24,768]{1,0:T(8,128)(2,1)}), bf16[768,768]{1,0:T(8,128)(2,1)}) %all-gather.14.cloned.1.call-update) | async-done | bytes 1179664 | tf_op jit(solution)/shard_map/all_gather | solution.py:140
  252.2 61.3 %all-gather.16.cloned.1.call-done = bf16[768,3072]{1,0:T(8,128)(2,1)} async-done(((bf16[24,3072]{1,0:T(8,128)(2,1)}), bf16[768,3072]{1,0:T(8,128)(2,1)}) %all-gather.16.cloned.1.call-update) | async-done | bytes 4718608 | tf_op jit(solution)/shard_map/all_gather | solution.py:141
  313.5 5.7 fusion.107
  321.5 11.6 multiply_convert_fusion
  333.1 45.6 %all-gather.18.cloned.1.call-done = bf16[3072,768]{1,0:T(8,128)(2,1)} async-done(((bf16[96,768]{1,0:T(8,128)(2,1)}), bf16[3072,768]{1,0:T(8,128)(2,1)}) %all-gather.18.cloned.1.call-update) | async-done | bytes 4718608 | tf_op jit(solution)/shard_map/all_gather | solution.py:142
  378.7 8.2 add_convert_fusion
  386.9 6.0 multiply_reduce_fusion.2
  398.4 3.5 all-to-all-start.6
  402.9 9.0 all-to-all-done.6
  411.9 4.3 fusion.142
  416.2 8.3 fusion.57
  424.6 2.5 copy.171
  427.1 4.4 fusion.60
  431.4 2.6 copy.172
  434.0 6.5 convolution_convert_fusion.1
  440.6 3.3 convolution_bitcast_fusion.3
  444.0 9.1 fusion.69
  453.2 17.0 %all_to_all.180 = bf16[12,128,1,192]{1,3,2,0:T(8,128)(2,1)S(1)} all-to-all(bf16[12,128,1,192]{1,3,2,0:T(8,128)(2,1)S(1)} %bitcast.237), channel_id=1, replica_groups=mesh['dp'=8,'seq'=4] {'seq'}, dimensions={0} | all-to-all | bytes 1179648 | tf_op jit(solution)/shard_map/all_to_all | solution.py:268
  480.4 4.7 convolution_bitcast_fusion.6
  486.6 2.7 broadcast_in_dim.91
  489.4 5.0 dynamic_update_slice.6
  494.3 4.8 dynamic_update_slice.7
  502.2 3.6 all-to-all-start.8
  507.2 8.1 all-to-all-done.8
  515.3 3.0 fusion.143
  518.4 4.6 fusion.75
  523.0 4.2 all-to-all-start.9
  527.2 4.5 fusion.78
  531.6 5.1 all-to-all-done.9
  536.8 4.1 all-to-all-start.10
  540.9 2.5 convolution_convert_fusion.2
  543.4 10.3 all-to-all-done.10
  553.7 3.5 all-to-all-start.11
  560.3 6.5 all-to-all-done.11
  567.0 5.1 convolution_bitcast_fusion
  573.5 6.9 convolution_bitcast_fusion.2
  581.5 8.0 convolution_bitcast_fusion.1
  589.5 6.0 fusion.72
  597.9 41.4 %all-reduce.6 = (f32[768]{0:T(1024)S(1)}, f32[768]{0:T(1024)S(1)}, f32[768]{0:T(1024)S(1)}) all-reduce(f32[768]{0:T(1024)S(1)} %get-tuple-element.19, f32[768]{0:T(1024)} %get-tuple-element.15, f32[768]{0:T(1024)} %get-tuple-element.17), channel_id=3, replica_groups=mesh['dp'=8,'seq'=4] {'dp','seq'}, use_global_device_ids=true, to_apply=%region_20.21.clone | all-reduce | flops 2304 | bytes 18432
  642.5 2.9 convert_element_type.174
  645.4 57.0 %reduce-scatter.15.cloned.1.call-done = f32[24,768]{1,0:T(8,128)} async-done(((f32[768,768]{1,0:T(8,128)}), f32[24,768]{1,0:T(8,128)}) %reduce-scatter.15.cloned.1.call-update) | async-done | bytes 73744 | tf_op jit(solution)/shard_map/reduce_scatter | solution.py:316
  702.4 104.8 %reduce-scatter.13.cloned.1.call-done = f32[24,768]{1,0:T(8,128)} async-done(((f32[768,768]{1,0:T(8,128)}), f32[24,768]{1,0:T(8,128)}) %reduce-scatter.13.cloned.1.call-update) | async-done | bytes 73744 | tf_op jit(solution)/shard_map/reduce_scatter | solution.py:315
  807.2 111.9 %reduce-scatter.17.cloned.1.call-done = f32[24,1536]{1,0:T(8,128)} async-done(((f32[768,1536]{1,0:T(8,128)}), f32[24,1536]{1,0:T(8,128)}) %reduce-scatter.17.cloned.1.call-update) | async-done | bytes 147472 | tf_op jit(solution)/shard_map/reduce_scatter | solution.py:317
  919.1 125.5 %reduce-scatter.11.cloned.1.call-done = f32[24,2304]{1,0:T(8,128)} async-done(((f32[768,2304]{1,0:T(8,128)}), f32[24,2304]{1,0:T(8,128)}) %reduce-scatter.11.cloned.1.call-update) | async-done | bytes 221200 | tf_op jit(solution)/shard_map/reduce_scatter | solution.py:314
  1044.6 141.1 %reduce-scatter.21.cloned.1.call-done = f32[24,3072]{1,0:T(8,128)} async-done(((f32[768,3072]{1,0:T(8,128)}), f32[24,3072]{1,0:T(8,128)}) %reduce-scatter.21.cloned.1.call-update) | async-done | bytes 294928 | tf_op jit(solution)/shard_map/reduce_scatter | solution.py:319
  1185.8 141.9 %reduce-scatter.23.cloned.1.call-done = f32[96,768]{1,0:T(8,128)} async-done(((f32[3072,768]{1,0:T(8,128)}), f32[96,768]{1,0:T(8,128)}) %reduce-scatter.23.cloned.1.call-update) | async-done | bytes 294928 | tf_op jit(solution)/shard_map/reduce_scatter | solution.py:320
  (247 shorter events, 86.1 us)
Async XLA Ops:
  7.2 66.8 %all-gather.8.cloned.1.call-start = ((), (), s32[]{:S(2)}) async-start(), calls=%async_computation.20 | async-start | bytes 3649536 | tf_op jit(solution)/shard_map/all_gather | solution.py:136
  7.9 125.7 %all-gather.12.cloned.1.call-start = ((), (), s32[]{:S(2)}) async-start(), calls=%async_computation.22 | async-start | bytes 2433024 | tf_op jit(solution)/shard_map/all_gather | solution.py:139
  8.7 183.7 %all-gather.10.cloned.1.call-start = ((), (), s32[]{:S(2)}) async-start(), calls=%async_computation.21 | async-start | bytes 1216512 | tf_op jit(solution)/shard_map/all_gather | solution.py:137
  9.4 238.8 %all-gather.14.cloned.1.call-start = ((), (), s32[]{:S(2)}) async-start(), calls=%async_computation.23 | async-start | bytes 1216512 | tf_op jit(solution)/shard_map/all_gather | solution.py:140
  10.0 303.5 %all-gather.16.cloned.1.call-start = ((), (), s32[]{:S(2)}) async-start(), calls=%async_computation.24 | async-start | bytes 4866048 | tf_op jit(solution)/shard_map/all_gather | solution.py:141
  10.6 368.2 %all-gather.18.cloned.1.call-start = ((), (), s32[]{:S(2)}) async-start(), calls=%async_computation.25 | async-start | bytes 4866048 | tf_op jit(solution)/shard_map/all_gather | solution.py:142
  58.6 19.3 %copy-start.48 = (f32[3,128]{1,0:T(4,128)}, f32[3,128]{1,0:T(4,128)S(1)}, u32[]{:S(2)}) copy-start(f32[3,128]{1,0:T(4,128)S(1)} %fusion.83) | copy-start | bytes 4612
  78.0 4.7 copy-start.33
  79.2 14.0 %all-to-all-start.2 = ((bf16[3,128,4,192]{1,3,0,2:T(8,128)(2,1)}), bf16[3,128,4,192]{1,3,0,2:T(8,128)(2,1)S(1)}, u32[]{:S(2)}, u32[]{:S(2)}) async-start(bf16[3,128,4,192]{1,3,0,2:T(8,128)(2,1)} %copy.140), calls=%async_computation.2 | async-start | bytes 1179648 | tf_op jit(solution)/shard_map/all_to_all | solution.py:170
  82.7 1.4 collective-permute-start
  84.1 12.6 collective-permute-start.1
  93.2 18.2 %copy-start.22 = (bf16[3,128,4,192]{1,3,0,2:T(8,128)(2,1)}, bf16[3,128,4,192]{1,3,0,2:T(8,128)(2,1)S(1)}, u32[]{:S(2)}) copy-start(bf16[3,128,4,192]{1,3,0,2:T(8,128)(2,1)S(1)} %all-to-all-done.2) | copy-start | bytes 1769476
  93.2 14.1 %all-to-all-start.1 = ((bf16[3,128,4,192]{1,3,0,2:T(8,128)(2,1)}), bf16[3,128,4,192]{1,3,0,2:T(8,128)(2,1)S(1)}, u32[]{:S(2)}, u32[]{:S(2)}) async-start(bf16[3,128,4,192]{1,3,0,2:T(8,128)(2,1)} %copy.138), calls=%async_computation.1 | async-start | bytes 1179648 | tf_op jit(solution)/shard_map/all_to_all | solution.py:169
  96.7 6.8 collective-permute-start.2
  98.2 97.0 %copy-start.34 = (f32[768]{0:T(1024)}, f32[768]{0:T(1024)S(1)}, u32[]{:S(2)}) copy-start(f32[768]{0:T(1024)S(1)} %convert_element_type.141) | copy-start | bytes 9220
  104.3 24.5 %collective-permute-start.3 = (bf16[192,768]{1,0:T(8,128)(2,1)}, bf16[192,768]{1,0:T(8,128)(2,1)}, u32[]{:S(2)}, u32[]{:S(2)}) collective-permute-start(bf16[192,768]{1,0:T(8,128)(2,1)} %maximum_select_fusion.2), channel_id=1, source_target_pairs={{0,8},{1,9},{2,10},{3,11},{4,12},{5,13},{6,14},{7,15},{8,0},{9,1},... | collective-permute-start | bytes 884744 | tf_op jit(solution)/shard_map/ppermute | solution.py:17
  107.2 5.5 copy-start.23
  107.2 14.9 %all-to-all-start = ((bf16[3,128,4,192]{1,3,0,2:T(8,128)(2,1)}), bf16[3,128,4,192]{1,3,0,2:T(8,128)(2,1)}, u32[]{:S(2)}, u32[]{:S(2)}) async-start(bf16[3,128,4,192]{1,3,0,2:T(8,128)(2,1)} %copy.136), calls=%async_computation | async-start | bytes 1179648 | tf_op jit(solution)/shard_map/all_to_all | solution.py:171
  112.8 11.8 copy-start.2
  113.8 10.7 copy-start.36
  122.1 6.1 copy-start.56
  124.5 67.8 %copy-start.1 = (bf16[3,128,768]{2,1,0:T(8,128)(2,1)S(1)}, bf16[3,128,768]{2,1,0:T(8,128)(2,1)}, u32[]{:S(2)}) copy-start(bf16[3,128,768]{2,1,0:T(8,128)(2,1)} %param.14) | copy-start | bytes 1769476
  124.5 13.1 all-to-all-start.3
  130.2 65.0 %collective-permute-start.4 = (bf16[384,768]{1,0:T(8,128)(2,1)S(1)}, bf16[384,768]{1,0:T(8,128)(2,1)}, u32[]{:S(2)}, u32[]{:S(2)}) collective-permute-start(bf16[384,768]{1,0:T(8,128)(2,1)S(1)} %maximum_select_fusion.1), channel_id=1, source_target_pairs={{0,16},{1,17},{2,18},{3,19},{4,20},{5,21},{6,22},{7,23},{8,24},{9,... | collective-permute-start | bytes 1769480 | tf_op jit(solution)/shard_map/ppermute | solution.py:17
  137.7 56.9 %copy-start.12 = (bf16[3,128,4,1,192]{1,4,2,0,3:T(8,128)(2,1)}, bf16[3,128,4,1,192]{1,4,2,0,3:T(8,128)(2,1)S(1)}, u32[]{:S(2)}) copy-start(bf16[3,128,4,1,192]{1,4,2,0,3:T(8,128)(2,1)S(1)} %copy.143) | copy-start | bytes 1769476
  197.8 5.6 copy-start.27
  198.2 5.2 copy-start.29
  199.0 14.1 %all-to-all-start.4 = ((bf16[3,128,4,192]{1,3,0,2:T(8,128)(2,1)}), bf16[3,128,4,192]{1,3,0,2:T(8,128)(2,1)}, u32[]{:S(2)}, u32[]{:S(2)}) async-start(bf16[3,128,4,192]{1,3,0,2:T(8,128)(2,1)} %copy.147), calls=%async_computation.4 | async-start | bytes 1179648 | tf_op jit(solution)/shard_map/all_to_all | solution.py:184
  209.2 4.0 copy-start.55
  215.9 4.0 copy-start
  215.9 4.0 copy-start.32
  218.1 6.0 copy-start.57
  219.8 13.0 all-to-all-start.5
  223.3 249.6 %all-gather.20.cloned.1.call-start = ((), (), s32[]{:S(2)}) async-start(), calls=%async_computation.26 | async-start | bytes 1216512 | tf_op jit(solution)/shard_map/all_gather | solution.py:211
  250.2 142.7 %copy-start.4 = (f32[3,128,768]{2,1,0:T(8,128)}, f32[3,128,768]{2,1,0:T(8,128)S(1)}, u32[]{:S(2)}) copy-start(f32[3,128,768]{2,1,0:T(8,128)S(1)} %get-tuple-element.47) | copy-start | bytes 3538948
  378.7 8.2 copy-start.40
  378.7 8.2 copy-start.44
  386.9 6.0 copy-start.25
  386.9 6.0 copy-start.53
  398.4 13.5 %all-to-all-start.6 = ((bf16[3,128,4,192]{1,3,0,2:T(8,128)(2,1)}), bf16[3,128,4,192]{1,3,0,2:T(8,128)(2,1)S(1)}, u32[]{:S(2)}, u32[]{:S(2)}) async-start(bf16[3,128,4,192]{1,3,0,2:T(8,128)(2,1)} %copy.153), calls=%async_computation.6 | async-start | bytes 1179648 | tf_op jit(solution)/shard_map/all_to_all | solution.py:242
  401.9 240.5 %reduce-scatter.9.cloned.1.call-start = ((), (), s32[]{:S(2)}) async-start(), calls=%async_computation.27 | async-start | bytes 5898240 | tf_op jit(solution)/shard_map/reduce_scatter | solution.py:258
  402.9 24.1 %copy-start.38 = (f32[12,3,128]{2,1,0:T(4,128)}, f32[12,3,128]{2,1,0:T(4,128)S(1)}, u32[]{:S(2)}) copy-start(f32[12,3,128]{2,1,0:T(4,128)S(1)} %log_add_fusion.1) | copy-start | bytes 55300
  440.5 204.8 %reduce-scatter.19.cloned.1.call-start = ((), (), s32[]{:S(2)}) async-start(), calls=%async_computation.32 | async-start | bytes 2433024 | tf_op jit(solution)/shard_map/reduce_scatter | solution.py:318
  443.9 258.5 %reduce-scatter.15.cloned.1.call-start = ((), (), s32[]{:S(2)}) async-start(), calls=%async_computation.30 | async-start | bytes 2433024 | tf_op jit(solution)/shard_map/reduce_scatter | solution.py:316
  453.1 17.1 %copy-start.35 = (f32[768]{0:T(1024)S(1)}, f32[768]{0:T(1024)}, u32[]{:S(2)}) copy-start(f32[768]{0:T(1024)} %copy-done.34) | copy-start | bytes 9220
  453.1 17.1 %copy-start.43 = (f32[3,128]{1,0:T(4,128)S(1)}, f32[3,128]{1,0:T(4,128)}, u32[]{:S(2)}) copy-start(f32[3,128]{1,0:T(4,128)} %copy-done.42) | copy-start | bytes 4612
  453.1 17.1 %copy-start.47 = (f32[3,128]{1,0:T(4,128)S(1)}, f32[3,128]{1,0:T(4,128)}, u32[]{:S(2)}) copy-start(f32[3,128]{1,0:T(4,128)} %copy-done.46) | copy-start | bytes 4612
  472.7 334.5 %reduce-scatter.13.cloned.1.call-start = ((), (), s32[]{:S(2)}) async-start(), calls=%async_computation.29 | async-start | bytes 2433024 | tf_op jit(solution)/shard_map/reduce_scatter | solution.py:315
  478.2 21.0 %copy-start.6 = (f32[3,128,768]{2,1,0:T(8,128)}, f32[3,128,768]{2,1,0:T(8,128)S(1)}, u32[]{:S(2)}) copy-start(f32[3,128,768]{2,1,0:T(8,128)S(1)} %add_add_fusion.4) | copy-start | bytes 3538948
  480.4 438.7 %reduce-scatter.17.cloned.1.call-start = ((), (), s32[]{:S(2)}) async-start(), calls=%async_computation.31 | async-start | bytes 4866048 | tf_op jit(solution)/shard_map/reduce_scatter | solution.py:317
  502.2 16.2 %copy-start.3 = (f32[12,3,128,128]{2,3,1,0:T(8,128)S(1)}, f32[12,3,128,128]{2,3,1,0:T(8,128)}, u32[]{:S(2)}) copy-start(f32[12,3,128,128]{2,3,1,0:T(8,128)} %copy-done.2) | copy-start | bytes 7077892
  502.2 13.1 all-to-all-start.8
  523.0 13.8 %all-to-all-start.9 = ((bf16[12,128,1,192]{1,3,2,0:T(8,128)(2,1)}), bf16[12,128,1,192]{1,3,2,0:T(8,128)(2,1)}, u32[]{:S(2)}, u32[]{:S(2)}) async-start(bf16[12,128,1,192]{1,3,2,0:T(8,128)(2,1)} %bitcast.236), calls=%async_computation.9 | async-start | bytes 1179648 | tf_op jit(solution)/shard_map/all_to_all | solution.py:288
  536.8 17.0 %all-to-all-start.10 = ((bf16[12,128,1,192]{1,3,2,0:T(8,128)(2,1)}), bf16[12,128,1,192]{1,3,2,0:T(8,128)(2,1)}, u32[]{:S(2)}, u32[]{:S(2)}) async-start(bf16[12,128,1,192]{1,3,2,0:T(8,128)(2,1)} %bitcast.235), calls=%async_computation.10 | async-start | bytes 1179648 | tf_op jit(solution)/shard_map/all_to_all | solution.py:291
  553.7 13.0 all-to-all-start.11
  557.2 487.4 %reduce-scatter.11.cloned.1.call-start = ((), (), s32[]{:S(2)}) async-start(), calls=%async_computation.28 | async-start | bytes 7299072 | tf_op jit(solution)/shard_map/reduce_scatter | solution.py:314
  560.2 11.9 copy-start.18
  567.0 5.1 copy-start.20
  572.2 613.5 %reduce-scatter.21.cloned.1.call-start = ((), (), s32[]{:S(2)}) async-start(), calls=%async_computation.33 | async-start | bytes 9732096 | tf_op jit(solution)/shard_map/reduce_scatter | solution.py:319
  580.4 747.3 %reduce-scatter.23.cloned.1.call-start = ((), (), s32[]{:S(2)}) async-start(), calls=%async_computation.34 | async-start | bytes 9732096 | tf_op jit(solution)/shard_map/reduce_scatter | solution.py:320
  589.5 6.1 copy-start.19
  589.5 6.1 copy-start.21
  589.5 6.1 copy-start.58
  597.2 43.8 %copy-start.7 = (f32[3,128,768]{2,1,0:T(8,128)S(1)}, f32[3,128,768]{2,1,0:T(8,128)}, u32[]{:S(2)}) copy-start(f32[3,128,768]{2,1,0:T(8,128)} %copy-done.6) | copy-start | bytes 3538948
  (26 other events, 45.0 us)
Sparse Core Ops, SparseCore 0:
  10.9 63.0 all-gather.7
  76.9 56.6 all-gather.11
  136.5 55.7 all-gather.9
  195.1 53.0 all-gather.13
  251.0 62.5 all-gather.15
  316.3 62.3 all-gather.17
  381.6 52.9 all-gather.19
  440.6 51.1 reduce-scatter.8
  498.6 100.0 reduce-scatter.18
  604.4 97.9 reduce-scatter.14
  709.1 98.0 reduce-scatter.12
  813.1 105.9 reduce-scatter.16
  926.3 118.2 reduce-scatter.10
  1051.0 134.7 reduce-scatter.20
  1193.1 134.5 reduce-scatter.22
